TPU v7x, 32 devices: a whole 2x2x4 slice. The times are simulated.
32 devices in a mesh: row: 8 (over y, x, core), col: 4 (over z).
Axes of the slice: x: 2, y: 2, z: 4, core: 2. Of those that a mesh axis runs over, the one named last changes fastest.
Arguments:
- gradient: bfloat16 [24576, 24576], P('row', 'col'), may hold values from -6 to 6
- sensitivity: bfloat16 [24576, 16384], P('row', 'col'), may hold values from -0.0390625 to 0.0390625
Outputs:
- influence: float32 [512, 16384], P('row', 'col')
All inputs are finite; a program needn't handle non-finite values.
Results may differ from a plain program's by a relative error of at most 0.0029.
Values may be sent and summed in bfloat16 or wider, within the bound.
A program may use at most 128 MiB of HBM per device.

v0:
```python
import jax
import jax.numpy as jnp
from jax import lax
from jax.sharding import PartitionSpec as P

PANEL = 512


def from_root(value, axis, root):
    mine = lax.axis_index(axis) == root
    return lax.psum(jnp.where(mine, value, jnp.zeros_like(value)), axis)


def shards(gradient, sensitivity):
    ratio = lax.axis_size("row") // lax.axis_size("col")
    own_panel = sensitivity[:, :PANEL]
    panel_here = from_root(own_panel, "col", 0)
    col_index = lax.axis_index("col")
    pieces = []
    for member in range(ratio):
        pieces.append(from_root(panel_here, "row", col_index * ratio + member))
    panel_block = jnp.concatenate(pieces, axis=0)
    partial_value = jnp.dot(gradient, panel_block, preferred_element_type=jnp.float32)
    image = lax.psum(partial_value, "col").astype(jnp.bfloat16)
    return lax.psum_scatter(
        lax.dot_general(
            image, sensitivity, (((0,), (0,)), ((), ())), preferred_element_type=jnp.float32
        ),
        "row",
        scatter_dimension=0,
        tiled=True,
    )


def solution(mesh):
    return jax.shard_map(
        shards,
        mesh=mesh,
        in_specs=(P("row", "col"), P("row", "col")),
        out_specs=P("row", "col"),
        check_vma=False,
    )
```

profile of v0, /device:TPU:0, one launch (start us, length us, event | category | flops | bytes accessed | tf_op | source)
XLA Modules:
  0.0 583.4 jit_solution(8317482870267149150)
XLA Ops:
  6.5 0.0 all-reduce.5.cloned.1.call-start
  6.5 3.8 slice_select_fusion
  10.3 0.0 all-reduce.5.cloned.1.call-update
  10.3 0.0 all-reduce.7.cloned.1.call-start
  10.4 123.9 %all-reduce.5.cloned.1.call-done = bf16[3072,512]{1,0:T(8,128)(2,1)} async-done(((bf16[3072,512]{1,0:T(8,128)(2,1)}), bf16[3072,512]{1,0:T(8,128)(2,1)}) %all-reduce.5.cloned.1.call-update) | async-done | bytes 3145744 | tf_op jit(solution)/shard_map/psum | solution.py:11
  134.3 5.0 broadcast_select_fusion.1
  139.2 0.0 all-reduce.7.cloned.1.call-update
  139.2 0.0 reduce-scatter.2.cloned.1.call-start
  139.3 103.5 %all-reduce.7.cloned.1.call-done = (bf16[3072,512]{1,0:T(8,128)(2,1)}, bf16[3072,512]{1,0:T(8,128)(2,1)}) async-done(((bf16[3072,512]{1,0:T(8,128)(2,1)}, bf16[3072,512]{1,0:T(8,128)(2,1)}), (bf16[3072,512]{1,0:T(8,128)(2,1)}, bf16[3072,512]{1,0:T(8,128)(2,1)})) %all-reduce.7.cloned.1.call-update) | async-done | bytes 6291472 | tf_op jit(solution)/shard_map/psum | solution.py:11
  242.8 27.1 %fusion.4 = f32[3072,512]{0,1:T(8,128)} fusion(bf16[3072,6144]{1,0:T(8,128)(2,1)} %param.2, bf16[3072,512]{1,0:T(8,128)(2,1)} %get-tuple-element.5, bf16[3072,512]{1,0:T(8,128)(2,1)} %get-tuple-element.6), kind=kOutput, calls=%fused_computation.4 | convolution fusion | flops 19339935744 | bytes 50331648 | tf_op jit(solution)/shard_map/dot_general | solution.py:23
  269.9 217.7 %all-reduce.8 = bf16[3072,512]{0,1:T(8,128)(2,1)S(1)} all-reduce(f32[3072,512]{0,1:T(8,128)} %fusion.4), channel_id=1, replica_groups=mesh['row'=8,'col'=4] {'col'}, use_global_device_ids=true, to_apply=%region_3.4 | all-reduce | flops 1572864 | bytes 9437184 | tf_op jit(solution)/shard_map/psum | solution.py:24
  487.5 19.9 %fusion.10 = f32[512,4096]{1,0:T(8,128)} fusion(bf16[3072,512]{0,1:T(8,128)(2,1)S(1)} %all-reduce.8, bf16[3072,4096]{1,0:T(8,128)(2,1)} %param.3), kind=kOutput, calls=%fused_computation.11 | convolution fusion | flops 12884901888 | bytes 36700160 | tf_op jit(solution)/shard_map/dot_general | solution.py:26
  507.4 0.0 reduce-scatter.2.cloned.1.call-update
  507.4 69.4 %reduce-scatter.2.cloned.1.call-done = f32[64,4096]{1,0:T(8,128)} async-done(((f32[512,4096]{1,0:T(8,128)}), f32[64,4096]{1,0:T(8,128)}) %reduce-scatter.2.cloned.1.call-update) | async-done | bytes 1048592 | tf_op jit(solution)/shard_map/reduce_scatter | solution.py:25
Async XLA Ops:
  6.5 127.7 %all-reduce.5.cloned.1.call-start = ((), (), s32[]{:S(2)}) async-start(), calls=%async_computation.1 | async-start | bytes 6291456 | tf_op jit(solution)/shard_map/psum | solution.py:11
  10.3 232.5 %all-reduce.7.cloned.1.call-start = ((), (), s32[]{:S(2)}) async-start(), calls=%async_computation.3 | async-start | bytes 12582912 | tf_op jit(solution)/shard_map/psum | solution.py:11
  139.2 437.6 %reduce-scatter.2.cloned.1.call-start = ((), (), s32[]{:S(2)}) async-start(), calls=%async_computation.2 | async-start | bytes 9437184 | tf_op jit(solution)/shard_map/reduce_scatter | solution.py:25
Sparse Core Ops, SparseCore 0:
  10.4 123.7 all-reduce.4
  139.4 103.3 all-reduce.6
  507.6 69.2 reduce-scatter.1
where the time goes:
time: 584 us; the launch traced here: 583 us
  waiting for transfers between devices  297 us (51%)
  blocking collectives  218 us (37%)
  matrix products  47 us (8%)
  between operations  13.1 us (2%)
  other arithmetic  8.71 us (1%)
    psum x2, waiting for transfers between devices, from_root(): return lax.psum(jnp.where(mine, value, jnp.zeros_like(value)), axis)  227 us
    psum x1, blocking collectives, shards(): image = lax.psum(partial_value, 'col').astype(jnp.bfloat16)  218 us
    reduce_scatter x1, waiting for transfers between devices, shards(): lax.psum_scatter(lax.dot_general(image, sensitivity, (((0,), (0,)), ((),...  69.4 us
    dot_general x1, matrix products, shards(): jnp.dot(gradient, panel_block, preferred_element_type=jnp.float32)  27.1 us
    dot_general x1, matrix products, shards(): lax.dot_general(image, sensitivity, (((0,), (0,)), ((), ())), preferred_e...  19.9 us
  transfers between devices with their start and end apart: 3, of which 3 were waited for; matrix products, arithmetic and copies ran while one was open for 0% of the time, Pallas kernels for 0%

commit v1 on v0

v1 whole, which is shorter than its diff:
```python
import functools

import jax
import jax.numpy as jnp
from jax import lax
from jax.experimental import pallas as pl
from jax.experimental.pallas import tpu as pltpu
from jax.sharding import PartitionSpec as P

PANEL = 512
TM = 256
TK = 768
TN = 512
MESH = pl.DeviceIdType.MESH


def kernel(R, C, grad, sens, out, panel, ybuf, own, rbuf, image, acc, sbuf, obuf, gbuf, vbuf, yacc, image_t,
           gsem, vsem, lsem, sc_s, sc_r, pg_s, pg_r, sb_s, sb_r, y_s, y_r, ag_s, ag_r, ps_s, ps_r, os_s, os_r):
    r, c = lax.axis_index("row"), lax.axis_index("col")
    ratio = R // C
    chips = R // 2
    core = lax.rem(r, 2)
    chip = r // 2
    sib = r + 1 - 2 * core
    rows, kdim = grad.shape
    width = sens.shape[1]
    T = rows // TM
    q = TM // C
    piece = kdim // R
    nsub = sc_r.shape[0]
    sub = piece // nsub
    po = PANEL // R

    def remote(src, dst, ssem, rsem, row, col):
        return pltpu.make_async_remote_copy(src_ref=src, dst_ref=dst, send_sem=ssem, recv_sem=rsem,
                                            device_id=(row, col), device_id_type=MESH)

    def load_g(t, slot):
        return pltpu.make_async_copy(grad.at[pl.ds(pl.multiple_of(t * TM, TM), TM)], gbuf.at[slot], gsem.at[slot])

    def load_v(t, slot):
        return pltpu.make_async_copy(sens.at[pl.ds(pl.multiple_of(t * TM, TM), TM)], vbuf.at[slot], vsem.at[slot])

    for t in range(min(2, T)):
        load_g(t, t).start()
        load_v(t, t).start()

    src_row = c * ratio + r // C
    self_fed = jnp.logical_and(c == 0, src_row == r)
    bar = pltpu.get_barrier_semaphore()
    for d in range(1, R):
        pl.semaphore_signal(bar, inc=1, device_id=(lax.rem(r + d, R), c), device_id_type=MESH)
    for d in range(1, C):
        pl.semaphore_signal(bar, inc=1, device_id=(r, lax.rem(c + d, C)), device_id_type=MESH)

    @pl.when(jnp.logical_not(self_fed))
    def _():
        pl.semaphore_signal(bar, inc=1, device_id=(src_row, 0), device_id_type=MESH)

    fed = jnp.where(c == 0, C, 0) - jnp.where(self_fed, 1, 0)
    pl.semaphore_wait(bar, R - 1 + C - 1 + fed)

    def prow(k, s):
        return panel.at[pl.ds(pl.multiple_of(k * piece + s * sub, sub), sub)]

    def scatter(j, s):
        k = lax.rem(r, ratio) * C + j
        src = sens.at[pl.ds(j * piece + s * sub, sub), pl.ds(0, PANEL)]
        return k, src, remote(src, prow(k, s), sc_s.at[j * nsub + s], sc_r.at[s], k, r // ratio)

    def is_self(j):
        return jnp.logical_and(r // ratio == 0, lax.rem(r, ratio) * C + j == r)

    def local(j, s):
        k, src, _ = scatter(j, s)
        return pltpu.make_async_copy(src, prow(k, s), lsem.at[s])

    @pl.when(c == 0)
    def _():
        for s in range(nsub):
            for j in range(C):
                @pl.when(is_self(j))
                def _():
                    local(j, s).start()

                @pl.when(jnp.logical_not(is_self(j)))
                def _():
                    scatter(j, s)[2].start()

    def gather(d, s):
        to = lax.rem(chip + d, chips) * 2 + core
        return remote(prow(r, s), prow(r, s), pg_s.at[(d - 1) * nsub + s], pg_r.at[(d - 1) * nsub + s], to, c)

    def to_sib(d, s):
        k = lax.rem(chip + chips - d, chips) * 2 + core
        return remote(prow(k, s), prow(k, s), sb_s.at[d * nsub + s], sb_r.at[d * nsub + s], sib, c)

    for s in range(nsub):
        @pl.when(self_fed)
        def _():
            local(0, s).wait()

        @pl.when(jnp.logical_not(self_fed))
        def _():
            remote(prow(r, s), prow(r, s), sc_s.at[s], sc_r.at[s], sib, c).wait_recv()

        for d in range(1, chips):
            gather(d, s).start()
        to_sib(0, s).start()
    for s in range(nsub):
        for d in range(1, chips):
            gather(d, s).wait_recv()
            to_sib(d, s).start()
    for s in range(nsub):
        for d in range(chips):
            to_sib(d, s).wait_recv()

    def y_copy(t, d):
        to = lax.rem(c + d, C)
        i = t * (C - 1) + d - 1
        return remote(ybuf.at[t, pl.ds(pl.multiple_of(to * q, q), q)], rbuf.at[i], y_s.at[i], y_r.at[i], r, to)

    def first(t, carry):
        slot = lax.rem(t, 2)
        load_g(t, slot).wait()
        yacc[...] = jnp.zeros_like(yacc)

        def step(k, carry):
            at = pl.ds(pl.multiple_of(k * TK, TK), TK)
            yacc[...] += jnp.dot(gbuf[slot, :, at], panel[at, :], preferred_element_type=jnp.float32)
            return carry

        lax.fori_loop(0, kdim // TK, step, 0)

        @pl.when(t + 2 < T)
        def _():
            load_g(t + 2, slot).start()

        ybuf[t] = yacc[...].astype(jnp.bfloat16)
        own[t] = yacc[pl.ds(pl.multiple_of(c * q, q), q), :]
        for d in range(1, C):
            y_copy(t, d).start()
        return carry

    lax.fori_loop(0, T, first, 0)
    acc[...] = jnp.zeros_like(acc)

    def ag(t, s, way):
        owner, to = (c - s, c + 1) if way == 0 else (c + s, c - 1)
        i = (t * (C - 1) + s) * 2 + way
        block = image.at[t, pl.ds(pl.multiple_of(owner * q, q), q)]
        return remote(block, block, ag_s.at[i], ag_r.at[i], r, to)

    def ag_cond(s, way):
        if way == 0:
            return jnp.logical_and(c - s >= 0, c + 1 < C)
        return jnp.logical_and(c + s < C, c - 1 >= 0)

    def ag_recv(t, s, way):
        owner = c - s if way == 0 else c + s
        i = (t * (C - 1) + s - 1) * 2 + way
        block = image.at[t, pl.ds(pl.multiple_of(owner * q, q), q)]
        return remote(block, block, ag_s.at[i], ag_r.at[i], r, lax.rem(c + 1, C))

    def send_on(t, s):
        for way in range(2):
            @pl.when(ag_cond(s, way))
            def _():
                ag(t, s, way).start()

    def second(u, carry):
        @pl.when(u < T)
        def _():
            total = own[u]
            for d in range(1, C):
                y_copy(u, d).wait_recv()
                total = total + rbuf[u * (C - 1) + d - 1].astype(jnp.float32)
            image[u, pl.ds(pl.multiple_of(c * q, q), q)] = total.astype(jnp.bfloat16)
            send_on(u, 0)

        for s in range(1, C):
            t = u - s

            @pl.when(jnp.logical_and(t >= 0, t < T))
            def _():
                @pl.when(c - s >= 0)
                def _():
                    ag_recv(t, s, 0).wait_recv()

                @pl.when(c + s < C)
                def _():
                    ag_recv(t, s, 1).wait_recv()

                if s < C - 1:
                    send_on(t, s)

        @pl.when(u >= C - 1)
        def _():
            t = u - (C - 1)
            slot = lax.rem(t, 2)
            load_v(t, slot).wait()
            image_t[...] = image[t].T

            def step(n, carry):
                at = pl.ds(pl.multiple_of(n * TN, TN), TN)
                acc[:, at] += jnp.dot(image_t[...], vbuf[slot, :, at], preferred_element_type=jnp.float32)
                return carry

            lax.fori_loop(0, width // TN, step, 0)

            @pl.when(t + 2 < T)
            def _():
                load_v(t + 2, slot).start()

        return carry

    lax.fori_loop(0, T + C - 1, second, 0)

    def arow(k):
        return acc.at[pl.ds(pl.multiple_of(k * po, po), po)]

    def pair(d):
        to = lax.rem(chip + d, chips)
        return remote(arow(to * 2 + 1 - core), sbuf.at[d], ps_s.at[d], ps_r.at[d], sib, c)

    def spread(d):
        k = lax.rem(chip + d, chips) * 2 + core
        return remote(arow(k), obuf.at[d - 1], os_s.at[d - 1], os_r.at[d - 1], k, c)

    order = list(range(1, chips)) + [0]
    for d in order:
        pair(d).start()
    for d in order:
        pair(d).wait_recv()
        k = lax.rem(chip + d, chips) * 2 + core
        at = pl.ds(pl.multiple_of(k * po, po), po)
        acc[at, :] += sbuf[d]
        if d:
            spread(d).start()
    mine = pl.ds(pl.multiple_of(r * po, po), po)
    for d in range(1, chips):
        spread(d).wait_recv()
        acc[mine, :] += obuf[d - 1]
    out[...] = acc[mine, :]

    @pl.when(c == 0)
    def _():
        for s in range(nsub):
            for j in range(C):
                @pl.when(jnp.logical_not(is_self(j)))
                def _():
                    scatter(j, s)[2].wait_send()

    for s in range(nsub):
        for d in range(1, chips):
            gather(d, s).wait_send()
        for d in range(chips):
            to_sib(d, s).wait_send()

    def drain(t, carry):
        for d in range(1, C):
            y_copy(t, d).wait_send()
        for s in range(C - 1):
            for way in range(2):
                @pl.when(ag_cond(s, way))
                def _():
                    ag(t, s, way).wait_send()
        return carry

    lax.fori_loop(0, T, drain, 0)
    for d in range(chips):
        pair(d).wait_send()
    for d in range(1, chips):
        spread(d).wait_send()


def shards(R, C, gradient, sensitivity):
    rows, kdim = gradient.shape
    width = sensitivity.shape[1]
    T, q, piece, po, chips = rows // TM, TM // C, kdim // R, PANEL // R, R // 2
    nsub = 4 if piece % 64 == 0 else 1
    dma = lambda n: pltpu.SemaphoreType.DMA((n,))
    return pl.pallas_call(
        functools.partial(kernel, R, C),
        out_shape=jax.ShapeDtypeStruct((po, width), jnp.float32),
        in_specs=[pl.BlockSpec(memory_space=pl.ANY)] * 2,
        out_specs=pl.BlockSpec(memory_space=pltpu.VMEM),
        scratch_shapes=[
            pltpu.VMEM((kdim, PANEL), jnp.bfloat16),
            pltpu.VMEM((T, TM, PANEL), jnp.bfloat16),
            pltpu.VMEM((T, q, PANEL), jnp.float32),
            pltpu.VMEM((T * (C - 1), q, PANEL), jnp.bfloat16),
            pltpu.VMEM((T, TM, PANEL), jnp.bfloat16),
            pltpu.VMEM((PANEL, width), jnp.float32),
            pltpu.VMEM((chips, po, width), jnp.float32),
            pltpu.VMEM((chips - 1, po, width), jnp.float32),
            pltpu.VMEM((2, TM, kdim), jnp.bfloat16),
            pltpu.VMEM((2, TM, width), jnp.bfloat16),
            pltpu.VMEM((TM, PANEL), jnp.float32),
            pltpu.VMEM((PANEL, TM), jnp.bfloat16),
            dma(2), dma(2), dma(nsub),
            dma(C * nsub), dma(nsub),
            dma((chips - 1) * nsub), dma((chips - 1) * nsub),
            dma(chips * nsub), dma(chips * nsub),
            dma(T * (C - 1)), dma(T * (C - 1)),
            dma(T * (C - 1) * 2), dma(T * (C - 1) * 2),
            dma(chips), dma(chips),
            dma(chips - 1), dma(chips - 1),
        ],
        compiler_params=pltpu.CompilerParams(
            collective_id=0, has_side_effects=True, vmem_limit_bytes=58 * 2**20
        ),
    )(gradient, sensitivity)


def solution(mesh):
    R, C = mesh.shape["row"], mesh.shape["col"]
    return jax.shard_map(
        functools.partial(shards, R, C),
        mesh=mesh,
        in_specs=(P("row", "col"), P("row", "col")),
        out_specs=P("row", "col"),
        check_vma=False,
    )
```

time: 584 us -> 265 us (0.45)
  waiting for transfers between devices: 297 us -> 0 us
  Pallas kernels: 0 us -> 262 us
  blocking collectives: 218 us -> 0 us
  matrix products: 47 us -> 0 us
  between operations: 13.1 us -> 0.01 us
  other arithmetic: 8.71 us -> 0 us
    pallas_call x0 -> x1, Pallas kernels: none -> 262 us  [shards(): pl.pallas_call(functools.partial(kernel, R, C), out_shape=jax.ShapeDtypeS...]
    psum x2 -> x0, waiting for transfers between devices: 227 us -> none  [from_root(): return lax.psum(jnp.where(mine, value, jnp.zeros_like(value)), axis)]
    psum x1 -> x0, blocking collectives: 218 us -> none  [shards(): image = lax.psum(partial_value, 'col').astype(jnp.bfloat16)]
    reduce_scatter x1 -> x0, waiting for transfers between devices: 69.4 us -> none  [shards(): lax.psum_scatter(lax.dot_general(image, sensitivity, (((0,), (0,)), ((),...]
    dot_general x2 -> x0, matrix products: 47 us -> none  [the longest x1 27.1 us: shards(): jnp.dot(gradient, panel_block, preferred_element_type=jnp.float32)]
    select_n x2 -> x0, other arithmetic: 8.71 us -> none  [from_root(): return lax.psum(jnp.where(mine, value, jnp.zeros_like(value)), axis)]
  transfers between devices with their start and end apart: 3 -> 0, of which waited for: 3 -> 0; matrix products, arithmetic and copies ran while one was open for 0% -> 0% of each run, Pallas kernels for 0% -> 0%
where the time goes in v1:
time: 265 us; the launch traced here: 264 us
  Pallas kernels  262 us (99%)
    pallas_call x1, Pallas kernels, shards(): pl.pallas_call(functools.partial(kernel, R, C), out_shape=jax.ShapeDtypeS...  262 us

profile of v1, /device:TPU:0, one launch (start us, length us, event | category | flops | bytes accessed | tf_op | source)
XLA Modules:
  0.0 264.0 jit_solution(4277367783562116634)
XLA Ops:
  0.0 261.7 %shard_map.28 = f32[64,4096]{1,0:T(8,128)} custom-call(bf16[3072,6144]{1,0:T(8,128)(2,1)} %grad.1, bf16[3072,4096]{1,0:T(8,128)(2,1)} %sens.1), custom_call_target="tpu_custom_call" | custom-call | tf_op jit(solution)/shard_map/pallas_call | solution.py:283
  261.7 2.3 copy.4

commit v2 on v1

v2 whole, which is shorter than its diff:
```python
import functools

import jax
import jax.numpy as jnp
from jax import lax
from jax.experimental import pallas as pl
from jax.experimental.pallas import tpu as pltpu
from jax.sharding import PartitionSpec as P

PANEL = 512
HALF = PANEL // 2
TK = 768
TN = 512
MESH = pl.DeviceIdType.MESH


def kernel(R, C, TM, grad, sens, source, out, panel, ybuf, own, rbuf, image, acc, sbuf, obuf, gbuf, vbuf, yacc, image_t,
           gsem, vsem, lsem, sc_s, sc_r, pg_s, pg_r, sb_s, sb_r, y_s, y_r, ag_s, ag_r, ps_s, ps_r, os_s, os_r):
    r, c = lax.axis_index("row"), lax.axis_index("col")
    ratio = R // C
    chips = R // 2
    core = lax.rem(r, 2)
    chip = r // 2
    sib = r + 1 - 2 * core
    rows, kdim = grad.shape
    width = sens.shape[1]
    T = rows // TM
    q = TM // C
    piece = kdim // R
    nsub = sc_r.shape[0] // 2
    sub = piece // nsub
    hp = PANEL // R // 2

    def remote(src, dst, ssem, rsem, row, col):
        return pltpu.make_async_remote_copy(src_ref=src, dst_ref=dst, send_sem=ssem, recv_sem=rsem,
                                            device_id=(row, col), device_id_type=MESH)

    def load(ref, buf, sem, tt):
        at = pl.ds(pl.multiple_of(lax.rem(tt, T) * TM, TM), TM)
        slot = lax.rem(tt, 2)
        return pltpu.make_async_copy(ref.at[at], buf.at[slot], sem.at[slot])

    def load_g(tt):
        return load(grad, gbuf, gsem, tt)

    def load_v(tt):
        return load(sens, vbuf, vsem, tt)

    for t in range(2):
        load_g(t).start()
        load_v(t).start()

    src_row = c * ratio + r // C
    self_fed = jnp.logical_and(c == 0, src_row == r)
    bar = pltpu.get_barrier_semaphore()
    for d in range(1, R):
        pl.semaphore_signal(bar, inc=1, device_id=(lax.rem(r + d, R), c), device_id_type=MESH)
    for d in range(1, C):
        pl.semaphore_signal(bar, inc=1, device_id=(r, lax.rem(c + d, C)), device_id_type=MESH)

    @pl.when(jnp.logical_not(self_fed))
    def _():
        pl.semaphore_signal(bar, inc=1, device_id=(src_row, 0), device_id_type=MESH)

    fed = jnp.where(c == 0, C, 0) - jnp.where(self_fed, 1, 0)
    pl.semaphore_wait(bar, R - 1 + C - 1 + fed)

    def prow(h, k, s):
        return panel.at[h, pl.ds(pl.multiple_of(k * piece + s * sub, sub), sub)]

    def source_at(h, j, s):
        return source.at[pl.ds(j * piece + s * sub, sub), pl.ds(h * HALF, HALF)]

    def scatter(h, j, s):
        k = lax.rem(r, ratio) * C + j
        i = h * nsub + s
        return remote(source_at(h, j, s), prow(h, k, s), sc_s.at[i * C + j], sc_r.at[i], k, r // ratio)

    def is_self(j):
        return jnp.logical_and(r // ratio == 0, lax.rem(r, ratio) * C + j == r)

    def local(h, j, s):
        k = lax.rem(r, ratio) * C + j
        return pltpu.make_async_copy(source_at(h, j, s), prow(h, k, s), lsem.at[h * nsub + s])

    @pl.when(c == 0)
    def _():
        for h in range(2):
            for s in range(nsub):
                for j in range(C):
                    @pl.when(is_self(j))
                    def _():
                        local(h, j, s).start()

                    @pl.when(jnp.logical_not(is_self(j)))
                    def _():
                        scatter(h, j, s).start()

    def gather(h, d, s):
        to = lax.rem(chip + d, chips) * 2 + core
        i = ((d - 1) * 2 + h) * nsub + s
        return remote(prow(h, r, s), prow(h, r, s), pg_s.at[i], pg_r.at[i], to, c)

    def to_sib(h, d, s):
        k = lax.rem(chip + chips - d, chips) * 2 + core
        i = (d * 2 + h) * nsub + s
        return remote(prow(h, k, s), prow(h, k, s), sb_s.at[i], sb_r.at[i], sib, c)

    def relay(h, s):
        @pl.when(self_fed)
        def _():
            local(h, 0, s).wait()

        @pl.when(jnp.logical_not(self_fed))
        def _():
            i = h * nsub + s
            remote(prow(h, r, s), prow(h, r, s), sc_s.at[i], sc_r.at[i], sib, c).wait_recv()

        for d in range(1, chips):
            gather(h, d, s).start()
        to_sib(h, 0, s).start()

    def relay_in(h, s):
        for d in range(1, chips):
            gather(h, d, s).wait_recv()
            to_sib(h, d, s).start()

    def complete(h):
        for s in range(nsub):
            for d in range(chips):
                to_sib(h, d, s).wait_recv()

    def y_copy(t, d):
        to = lax.rem(c + d, C)
        i = t * (C - 1) + d - 1
        return remote(ybuf.at[t, pl.ds(pl.multiple_of(to * q, q), q)], rbuf.at[i], y_s.at[i], y_r.at[i], r, to)

    def first(h, t, carry):
        tt = h * T + t
        slot = lax.rem(tt, 2)
        load_g(tt).wait()
        yacc[...] = jnp.zeros_like(yacc)

        def step(k, carry):
            at = pl.ds(pl.multiple_of(k * TK, TK), TK)
            yacc[...] += jnp.dot(gbuf[slot, :, at], panel[h, at, :], preferred_element_type=jnp.float32)
            return carry

        lax.fori_loop(0, kdim // TK, step, 0)

        @pl.when(tt + 2 < 2 * T)
        def _():
            load_g(tt + 2).start()

        ybuf[tt] = yacc[...].astype(jnp.bfloat16)
        own[tt] = yacc[pl.ds(pl.multiple_of(c * q, q), q), :]
        for d in range(1, C):
            y_copy(tt, d).start()
        return carry

    def ag(t, s, way):
        owner, to = (c - s, c + 1) if way == 0 else (c + s, c - 1)
        i = (t * (C - 1) + s) * 2 + way
        block = image.at[t, pl.ds(pl.multiple_of(owner * q, q), q)]
        return remote(block, block, ag_s.at[i], ag_r.at[i], r, to)

    def ag_cond(s, way):
        if way == 0:
            return jnp.logical_and(c - s >= 0, c + 1 < C)
        return jnp.logical_and(c + s < C, c - 1 >= 0)

    def ag_recv(t, s, way):
        owner = c - s if way == 0 else c + s
        i = (t * (C - 1) + s - 1) * 2 + way
        block = image.at[t, pl.ds(pl.multiple_of(owner * q, q), q)]
        return remote(block, block, ag_s.at[i], ag_r.at[i], r, lax.rem(c + 1, C))

    def send_on(t, s):
        for way in range(2):
            @pl.when(ag_cond(s, way))
            def _():
                ag(t, s, way).start()

    def second(h, u, carry):
        @pl.when(u < T)
        def _():
            tt = h * T + u
            total = own[tt]
            for d in range(1, C):
                y_copy(tt, d).wait_recv()
                total = total + rbuf[tt * (C - 1) + d - 1].astype(jnp.float32)
            image[tt, pl.ds(pl.multiple_of(c * q, q), q)] = total.astype(jnp.bfloat16)
            send_on(tt, 0)

        for s in range(1, C):
            t = u - s

            @pl.when(jnp.logical_and(t >= 0, t < T))
            def _():
                tt = h * T + t

                @pl.when(c - s >= 0)
                def _():
                    ag_recv(tt, s, 0).wait_recv()

                @pl.when(c + s < C)
                def _():
                    ag_recv(tt, s, 1).wait_recv()

                if s < C - 1:
                    send_on(tt, s)

        @pl.when(u >= C - 1)
        def _():
            tt = h * T + u - (C - 1)
            slot = lax.rem(tt, 2)
            load_v(tt).wait()
            image_t[...] = image[tt].T

            def step(n, carry):
                at = pl.ds(pl.multiple_of(n * TN, TN), TN)
                acc[h, :, at] += jnp.dot(image_t[...], vbuf[slot, :, at], preferred_element_type=jnp.float32)
                return carry

            lax.fori_loop(0, width // TN, step, 0)

            @pl.when(tt + 2 < 2 * T)
            def _():
                load_v(tt + 2).start()

        return carry

    def arow(h, k):
        return acc.at[h, pl.ds(pl.multiple_of(k * hp, hp), hp)]

    def pair(h, d):
        to = lax.rem(chip + d, chips)
        i = h * chips + d
        return remote(arow(h, to * 2 + 1 - core), sbuf.at[i], ps_s.at[i], ps_r.at[i], sib, c)

    def spread(h, d):
        k = lax.rem(chip + d, chips) * 2 + core
        i = h * (chips - 1) + d - 1
        return remote(arow(h, k), obuf.at[i], os_s.at[i], os_r.at[i], k, c)

    order = list(range(1, chips)) + [0]

    def out_pair(h):
        for d in order:
            pair(h, d).start()

    def out_spread(h):
        for d in order:
            pair(h, d).wait_recv()
            k = lax.rem(chip + d, chips) * 2 + core
            at = pl.ds(pl.multiple_of(k * hp, hp), hp)
            acc[h, at, :] += sbuf[h * chips + d]
            if d:
                spread(h, d).start()

    def out_sum(h):
        total = acc[h, pl.ds(pl.multiple_of(r * hp, hp), hp), :]
        for d in range(1, chips):
            spread(h, d).wait_recv()
            total = total + obuf[h * (chips - 1) + d - 1]
        out[pl.ds(h * hp, hp), :] = total

    for s in range(nsub):
        relay(0, s)
    for s in range(nsub):
        relay_in(0, s)
    complete(0)
    for s in range(nsub):
        relay(1, s)
        lax.fori_loop(T * s // nsub, T * (s + 1) // nsub, functools.partial(first, 0), 0)
        if s:
            relay_in(1, s - 1)
    relay_in(1, nsub - 1)
    complete(1)
    lax.fori_loop(0, T, functools.partial(first, 1), 0)
    acc[...] = jnp.zeros_like(acc)
    steps = T + C - 1
    lax.fori_loop(0, steps, functools.partial(second, 0), 0)
    out_pair(0)
    lax.fori_loop(0, 1, functools.partial(second, 1), 0)
    out_spread(0)
    lax.fori_loop(1, steps, functools.partial(second, 1), 0)
    out_pair(1)
    out_sum(0)
    out_spread(1)
    out_sum(1)

    for h in range(2):
        @pl.when(c == 0)
        def _():
            for s in range(nsub):
                for j in range(C):
                    @pl.when(jnp.logical_not(is_self(j)))
                    def _():
                        scatter(h, j, s).wait_send()

        for s in range(nsub):
            for d in range(1, chips):
                gather(h, d, s).wait_send()
            for d in range(chips):
                to_sib(h, d, s).wait_send()

    def drain(t, carry):
        for d in range(1, C):
            y_copy(t, d).wait_send()
        for s in range(C - 1):
            for way in range(2):
                @pl.when(ag_cond(s, way))
                def _():
                    ag(t, s, way).wait_send()
        return carry

    lax.fori_loop(0, 2 * T, drain, 0)
    for h in range(2):
        for d in range(chips):
            pair(h, d).wait_send()
        for d in range(1, chips):
            spread(h, d).wait_send()


def shards(R, C, gradient, sensitivity):
    rows, kdim = gradient.shape
    width = sensitivity.shape[1]
    TM = 512 if rows % 512 == 0 else 256
    T, q, piece, po, chips = rows // TM, TM // C, kdim // R, PANEL // R, R // 2
    hp = po // 2
    nsub = 4 if piece % 64 == 0 else 1
    n = jnp.arange(PANEL)
    h, k, i = n // HALF, n % HALF // hp, n % hp
    taken = k * po + h * hp + i
    pick = (jnp.arange(PANEL)[:, None] == taken[None, :]).astype(jnp.bfloat16)
    source = jnp.dot(sensitivity[:, :PANEL], pick, preferred_element_type=jnp.bfloat16)
    dma = lambda n: pltpu.SemaphoreType.DMA((n,))
    return pl.pallas_call(
        functools.partial(kernel, R, C, TM),
        out_shape=jax.ShapeDtypeStruct((po, width), jnp.float32),
        in_specs=[pl.BlockSpec(memory_space=pl.ANY)] * 3,
        out_specs=pl.BlockSpec(memory_space=pltpu.VMEM),
        scratch_shapes=[
            pltpu.VMEM((2, kdim, HALF), jnp.bfloat16),
            pltpu.VMEM((2 * T, TM, HALF), jnp.bfloat16),
            pltpu.VMEM((2 * T, q, HALF), jnp.float32),
            pltpu.VMEM((2 * T * (C - 1), q, HALF), jnp.bfloat16),
            pltpu.VMEM((2 * T, TM, HALF), jnp.bfloat16),
            pltpu.VMEM((2, HALF, width), jnp.float32),
            pltpu.VMEM((2 * chips, hp, width), jnp.float32),
            pltpu.VMEM((2 * (chips - 1), hp, width), jnp.float32),
            pltpu.VMEM((2, TM, kdim), jnp.bfloat16),
            pltpu.VMEM((2, TM, width), jnp.bfloat16),
            pltpu.VMEM((TM, HALF), jnp.float32),
            pltpu.VMEM((HALF, TM), jnp.bfloat16),
            dma(2), dma(2), dma(2 * nsub),
            dma(2 * C * nsub), dma(2 * nsub),
            dma(2 * (chips - 1) * nsub), dma(2 * (chips - 1) * nsub),
            dma(2 * chips * nsub), dma(2 * chips * nsub),
            dma(2 * T * (C - 1)), dma(2 * T * (C - 1)),
            dma(4 * T * (C - 1)), dma(4 * T * (C - 1)),
            dma(2 * chips), dma(2 * chips),
            dma(2 * (chips - 1)), dma(2 * (chips - 1)),
        ],
        compiler_params=pltpu.CompilerParams(
            collective_id=0, has_side_effects=True, vmem_limit_bytes=60 * 2**20
        ),
    )(gradient, sensitivity, source)


def solution(mesh):
    R, C = mesh.shape["row"], mesh.shape["col"]
    return jax.shard_map(
        functools.partial(shards, R, C),
        mesh=mesh,
        in_specs=(P("row", "col"), P("row", "col")),
        out_specs=P("row", "col"),
        check_vma=False,
    )
```

time: 265 us -> 245 us (0.925)
  Pallas kernels: 262 us -> 237 us
  matrix products: 0 us -> 5.4 us
    pallas_call x1, Pallas kernels: 262 us -> 237 us  [shards(): pl.pallas_call(functools.partial(kernel, R, C, TM), out_shape=jax.ShapeDt...]
    dot_general x0 -> x1, matrix products: none -> 5.4 us  [shards(): jnp.dot(sensitivity[:, :PANEL], pick, preferred_element_type=jnp.bfloat16)]
where the time goes in v2:
time: 245 us; the launch traced here: 244 us
  Pallas kernels  237 us (97%)
  matrix products  5.4 us (2%)
    pallas_call x1, Pallas kernels, shards(): pl.pallas_call(functools.partial(kernel, R, C, TM), out_shape=jax.ShapeDt...  237 us
    dot_general x1, matrix products, shards(): jnp.dot(sensitivity[:, :PANEL], pick, preferred_element_type=jnp.bfloat16)  5.4 us

profile of v2, /device:TPU:0, one launch (start us, length us, event | category | flops | bytes accessed | tf_op | source)
XLA Modules:
  0.0 244.3 jit_solution(992980330365867734)
XLA Ops:
  0.0 5.4 %convolution_bitcast_fusion.source = bf16[3072,512]{1,0:T(8,128)(2,1)} fusion(bf16[3072,4096]{1,0:T(8,128)(2,1)} %sens.1, s32[512]{0:T(512)S(1)} %fusion.13), kind=kOutput, calls=%fused_computation | convolution fusion | flops 1610874880 | bytes 6293504 | tf_op jit(solution)/shard_map/dot_general | solution.py:337
  5.4 236.7 %shard_map.28 = f32[64,4096]{1,0:T(8,128)} custom-call(bf16[3072,6144]{1,0:T(8,128)(2,1)} %grad.1, bf16[3072,4096]{1,0:T(8,128)(2,1)} %sens.1, bf16[3072,512]{1,0:T(8,128)(2,1)} %convolution_bitcast_fusion.source), custom_call_target="tpu_custom_call" | custom-call | tf_op jit(solution)/shard_map/pallas_call | solution.py:339
  242.1 2.3 copy.6
  (1 shorter events, 0.0 us)

commit v3 on v2

--- a/solution.py
+++ b/solution.py
@@ -265,10 +265,12 @@
             total = total + obuf[h * (chips - 1) + d - 1]
         out[pl.ds(h * hp, hp), :] = total
 
+    acc[...] = jnp.zeros_like(acc)
     for s in range(nsub):
         relay(0, s)
-    for s in range(nsub):
-        relay_in(0, s)
+        if s:
+            relay_in(0, s - 1)
+    relay_in(0, nsub - 1)
     complete(0)
     for s in range(nsub):
         relay(1, s)
@@ -277,10 +279,13 @@
             relay_in(1, s - 1)
     relay_in(1, nsub - 1)
     complete(1)
-    lax.fori_loop(0, T, functools.partial(first, 1), 0)
-    acc[...] = jnp.zeros_like(acc)
     steps = T + C - 1
-    lax.fori_loop(0, steps, functools.partial(second, 0), 0)
+
+    def both(t, carry):
+        return second(0, t, first(1, t, carry))
+
+    lax.fori_loop(0, T, both, 0)
+    lax.fori_loop(T, steps, functools.partial(second, 0), 0)
     out_pair(0)
     lax.fori_loop(0, 1, functools.partial(second, 1), 0)
     out_spread(0)

time: 245 us -> 243 us (level)
  no operation moved by 1% of the time
where the time goes in v3:
time: 243 us
  Pallas kernels  235 us (97%)
  matrix products  5.4 us (2%)
    pallas_call x1, Pallas kernels, shards(): pl.pallas_call(functools.partial(kernel, R, C, TM), out_shape=jax.ShapeDt...  235 us
    dot_general x1, matrix products, shards(): jnp.dot(sensitivity[:, :PANEL], pick, preferred_element_type=jnp.bfloat16)  5.4 us

profile of v3, /device:TPU:0, one launch (start us, length us, event | category | flops | bytes accessed | tf_op | source)
XLA Modules:
  0.0 242.5 jit_solution(6890723062871756309)
XLA Ops:
  0.0 5.4 %convolution_bitcast_fusion.source = bf16[3072,512]{1,0:T(8,128)(2,1)} fusion(bf16[3072,4096]{1,0:T(8,128)(2,1)} %sens.1, s32[512]{0:T(512)S(1)} %fusion.13), kind=kOutput, calls=%fused_computation | convolution fusion | flops 1610874880 | bytes 6293504 | tf_op jit(solution)/shard_map/dot_general | solution.py:342
  5.4 234.8 %shard_map.28 = f32[64,4096]{1,0:T(8,128)} custom-call(bf16[3072,6144]{1,0:T(8,128)(2,1)} %grad.1, bf16[3072,4096]{1,0:T(8,128)(2,1)} %sens.1, bf16[3072,512]{1,0:T(8,128)(2,1)} %convolution_bitcast_fusion.source), custom_call_target="tpu_custom_call" | custom-call | tf_op jit(solution)/shard_map/pallas_call | solution.py:344
  240.2 2.3 copy.6
  (1 shorter events, 0.0 us)
